TPU v7x, 256 devices: a whole 4x4x8 slice. The times are simulated.
256 devices in a mesh: tm: 32 (over y_lo, z, core), gy: 8 (over y_hi, x).
Axes of the slice: x: 4, y: 4 (y_hi: 2, y_lo: 2; y = y_hi * 2 + y_lo), z: 8, core: 2. Of those that a mesh axis runs over, the one named last changes fastest.
Arguments:
- magnetic: bfloat16 [32, 3, 3, 1024, 1024], P('tm', None, None, 'gy'), may hold values from -6 to 6
- velocity: bfloat16 [32, 3, 1, 1024, 1024], P('tm', None, None, 'gy'), may hold values from -6 to 6
- mode_bin: int32 [1024, 1024], P(None, 'gy'), may hold values from 0 to 127, as said below
- omega_edges: int32 [9], replicated, may hold values from 0 to 32, as said below
Outputs:
- power: float32 [32, 1024, 1024], P('tm', None, 'gy')
- spectrum: float32 [8, 128], replicated
Inputs may be any that keep to these rules, and one draw needn't show every extreme that they name: mode_bin = 16 * p + q, where p is a level of min(kz, 1024 - kz) and q a level of min(ky, 1024 - ky); levels never fall as the wavenumber rises, and every value occurs. `omega_edges`: edges rise strictly, the first 0 and the last 32.
All inputs are finite; a program needn't handle non-finite values.
Results may differ from a plain program's by a relative error of at most 0.004.
The roundings to bfloat16 on the way count: a program that leaves them out, or rounds other values in their place, can miss the bound.
Values may be sent and summed in bfloat16 or wider, within the bound.
No kernel may reach another device: no remote copies, remote signals or barrier semaphores. Data moves between devices by JAX's collectives and lax.ppermute only.
A program may use at most 128 MiB of HBM per device.

v0:
```python
import math
import jax
import jax.numpy as jnp
from jax import lax
from jax.sharding import PartitionSpec as P

NBP = 8
NBQ = 16
NB_W = 8
hall_coef = 1.0
highest = lax.Precision.HIGHEST


def extended(cells, sides, width):
    for axis, dim in sides:
        count = lax.axis_size(axis)
        head = lax.slice_in_dim(cells, 0, width, axis=dim)
        tail = lax.slice_in_dim(cells, cells.shape[dim] - width, cells.shape[dim], axis=dim)
        cells = jnp.concatenate(
            [
                lax.ppermute(tail, axis, [(i, (i + 1) % count) for i in range(count)]),
                cells,
                lax.ppermute(head, axis, [((i + 1) % count, i) for i in range(count)]),
            ],
            axis=dim,
        )
    return cells


def window_taper_for(sample_moments, every_time_sample):
    return 0.5 - 0.5 * jnp.cos(
        2.0 * math.pi * (sample_moments.astype(jnp.float32) + 0.5) / every_time_sample
    )


def temporal_coefficients(angular_frequency, sample_moments, every_time_sample):
    phase_angles = jnp.mod(
        angular_frequency[:, None] * sample_moments[None, :], every_time_sample
    ).astype(jnp.float32)
    angles = 2.0 * math.pi * phase_angles / every_time_sample
    taper_weight = window_taper_for(sample_moments, every_time_sample)[None, :]
    return (
        (taper_weight * jnp.cos(angles)).astype(jnp.bfloat16),
        (-taper_weight * jnp.sin(angles)).astype(jnp.bfloat16),
    )


def dft_tables(length):
    series = jnp.arange(length, dtype=jnp.int32)
    phase_angles = jnp.mod(series[:, None] * series[None, :], length).astype(jnp.float32)
    angles = 2.0 * math.pi * phase_angles / length
    return (jnp.cos(angles).astype(jnp.bfloat16), jnp.sin(angles).astype(jnp.bfloat16))


def z_slope(values):
    return (jnp.roll(values, -1, axis=-1) - jnp.roll(values, 1, axis=-1)) * 0.5


def z_turn(re_part, im_part):
    zcos_tab, zsin_tab = dft_tables(re_part.shape[-1])
    turned_re = jnp.dot(re_part, zcos_tab, preferred_element_type=jnp.float32) + jnp.dot(
        im_part, zsin_tab, preferred_element_type=jnp.float32
    )
    turned_im = jnp.dot(im_part, zcos_tab, preferred_element_type=jnp.float32) - jnp.dot(
        re_part, zsin_tab, preferred_element_type=jnp.float32
    )
    return jnp.stack([turned_re, turned_im]).astype(jnp.bfloat16)


def electric_of(magnetic, velocity, slope_magz, slope_magx):
    inner = magnetic[:, :, 1:-1].astype(jnp.float32)
    x_slope = (
        magnetic[:, :, 2:].astype(jnp.float32) - magnetic[:, :, :-2].astype(jnp.float32)
    ) * 0.5
    mag_x, mag_y, mag_z = (inner[:, 0], inner[:, 1], inner[:, 2])
    cur_x = slope_magz - z_slope(mag_y)
    cur_y = z_slope(mag_x) - x_slope[:, 2]
    cur_z = x_slope[:, 1] - slope_magx
    flow = velocity.astype(jnp.float32)
    vel_x, vel_y, vel_z = (flow[:, 0], flow[:, 1], flow[:, 2])
    elec_x = -(vel_y * mag_z - vel_z * mag_y) + hall_coef * (cur_y * mag_z - cur_z * mag_y)
    elec_y = -(vel_z * mag_x - vel_x * mag_z) + hall_coef * (cur_z * mag_x - cur_x * mag_z)
    elec_z = -(vel_x * mag_y - vel_y * mag_x) + hall_coef * (cur_x * mag_y - cur_y * mag_x)
    return jnp.stack([elec_x, elec_y, elec_z], axis=1)


def body(magnetic, velocity, mode_bin, omega_edges):
    face_rows = jnp.stack([magnetic[:, 2, 1:-1], magnetic[:, 0, 1:-1]], axis=1)
    padded = extended(face_rows, (("gy", 3),), 1)
    slopes = (
        padded[:, :, :, 2:].astype(jnp.float32) - padded[:, :, :, :-2].astype(jnp.float32)
    ) * 0.5
    electric = electric_of(magnetic, velocity, slopes[:, 0], slopes[:, 1]).astype(jnp.bfloat16)
    local_t = electric.shape[0]
    z_count = electric.shape[-1]
    every_time_sample = local_t * lax.axis_size("tm")
    half_count = every_time_sample // 2
    owner_rank = lax.axis_index("tm")
    angular_frequency = owner_rank * local_t + jnp.arange(local_t, dtype=jnp.int32) - half_count
    time_segment = lax.all_gather(electric, "tm", axis=0, tiled=True)
    sample_moments = jnp.arange(time_segment.shape[0], dtype=jnp.int32)
    coefficient_real, coefficient_imaginary = temporal_coefficients(
        angular_frequency, sample_moments, every_time_sample
    )
    re_part = jnp.einsum(
        "wt,tcxyz->wcxyz", coefficient_real, time_segment, preferred_element_type=jnp.float32
    )
    im_part = jnp.einsum(
        "wt,tcxyz->wcxyz", coefficient_imaginary, time_segment, preferred_element_type=jnp.float32
    )
    moved = lax.all_to_all(
        z_turn(re_part.astype(jnp.bfloat16), im_part.astype(jnp.bfloat16)),
        "gy",
        split_axis=5,
        concat_axis=4,
        tiled=True,
    )
    y_count = moved.shape[4]
    ycos_tab, ysin_tab = dft_tables(y_count)
    wave_re = jnp.einsum(
        "wcxyk,yq->wcxqk", moved[0], ycos_tab, preferred_element_type=jnp.float32
    ) + jnp.einsum("wcxyk,yq->wcxqk", moved[1], ysin_tab, preferred_element_type=jnp.float32)
    wave_im = jnp.einsum(
        "wcxyk,yq->wcxqk", moved[1], ycos_tab, preferred_element_type=jnp.float32
    ) - jnp.einsum("wcxyk,yq->wcxqk", moved[0], ysin_tab, preferred_element_type=jnp.float32)
    power_map = jnp.sum(wave_re * wave_re + wave_im * wave_im, axis=(1, 2)) / (
        every_time_sample * y_count * z_count
    )
    kz_local = power_map.shape[2]
    block_rows = min(64, y_count)
    bin_total = NBP * NBQ
    bin_range = jnp.arange(bin_total, dtype=jnp.int32)

    def add_block(step_num, summed):
        row_block = lax.dynamic_slice_in_dim(
            power_map, step_num * block_rows, block_rows, 1
        ).reshape(local_t, block_rows * kz_local)
        bin_ids = lax.dynamic_slice_in_dim(mode_bin, step_num * block_rows, block_rows, 0).reshape(
            block_rows * kz_local
        )
        onehot = (bin_ids[:, None] == bin_range[None, :]).astype(jnp.float32)
        return summed + jnp.dot(row_block, onehot, precision=highest)

    by_mode = lax.fori_loop(
        0, y_count // block_rows, add_block, jnp.zeros((local_t, bin_total), jnp.float32)
    )
    omega = owner_rank * local_t + jnp.arange(local_t, dtype=jnp.int32)
    member = (
        (omega[None, :] >= omega_edges[:-1, None]) & (omega[None, :] < omega_edges[1:, None])
    ).astype(jnp.float32)
    partial_value = jnp.dot(member, by_mode, precision=highest)
    binned = lax.psum(partial_value, ("tm", "gy"))
    spectrum = jnp.log(
        binned * (NB_W * bin_total) / (every_time_sample * y_count * z_count) + 1e-06
    )
    return (power_map, spectrum)


def solution(mesh):
    return jax.shard_map(
        body,
        mesh=mesh,
        in_specs=(
            P("tm", None, None, "gy", None),
            P("tm", None, None, "gy", None),
            P(None, "gy"),
            P(),
        ),
        out_specs=(P("tm", None, "gy"), P()),
        check_vma=False,
    )
```

profile of v0, /device:TPU:1, one launch (start us, length us, event | category | flops | bytes accessed | tf_op | source)
XLA Modules:
  0.0 512.5 jit_solution(18000967554781323091)
XLA Ops:
  8.5 6.0 %collective-permute-start = (bf16[1,2,1,1,1024]{4,3,2,1,0:T(2,128)(2,1)S(1)}, bf16[1,2,1,1,1024]{4,3,2,1,0:T(2,128)(2,1)S(1)}, u32[]{:S(2)}, u32[]{:S(2)}) collective-permute-start(bf16[1,2,1,1,1024]{4,3,2,1,0:T(2,128)(2,1)S(1)} %get-tuple-element.139), channel_id=1, source_target_pairs={{1,0},{2,1},{3,2},{4,3},{5,4},{6,5},{7,6},{0,7},{9,8},{10,9},{11,1... | collective-permute-start | bytes 12296 | tf_op jit(solution)/shard_map/ppermute | solution.py:23
  16.7 3.9 collective-permute-done.1
  23.7 142.3 %all-gather.2.cloned.1.call-done = bf16[32,3,1,128,1024]{4,3,2,1,0:T(8,128)(2,1)} async-done(((bf16[1,3,1,128,1024]{4,3,2,1,0:T(8,128)(2,1)}), bf16[32,3,1,128,1024]{4,3,2,1,0:T(8,128)(2,1)}) %all-gather.2.cloned.1.call-update) | async-done | bytes 25165840 | tf_op jit(solution)/shard_map/all_gather | solution.py:100
  166.0 24.4 %fusion.5 = bf16[1,3,128,1024]{3,0,2,1:T(2,128)(2,1)S(1)} fusion(bf16[32,3,128,1024]{3,2,1,0:T(8,128)(2,1)} %bitcast.97, s32[]{:T(128)S(6)} %sub.139), kind=kOutput, calls=%fused_computation.8 | convolution fusion | flops 25166528 | bytes 25952260 | tf_op jit(solution)/shard_map/wt,tcxyz->wcxyz/dot_general | solution.py:108
  190.5 24.9 %fusion.7 = bf16[1,3,128,1024]{3,0,2,1:T(2,128)(2,1)S(1)} fusion(bf16[32,3,128,1024]{3,2,1,0:T(8,128)(2,1)} %bitcast.98, s32[]{:T(128)S(6)} %sub.139), kind=kOutput, calls=%fused_computation.10 | convolution fusion | flops 25166496 | bytes 25952260 | tf_op jit(solution)/shard_map/wt,tcxyz->wcxyz/dot_general | solution.py:105
  215.4 16.1 %fusion.21 = f32[3,128,1024]{2,1,0:T(8,128)S(1)} fusion(bf16[1,3,128,1024]{3,0,2,1:T(2,128)(2,1)S(1)} %fusion.7), kind=kOutput, calls=%fused_computation.27 | convolution fusion | flops 821035008 | bytes 2359296 | tf_op jit(solution)/shard_map/dot_general | solution.py:64
  231.5 16.1 %fusion.23 = f32[3,128,1024]{2,1,0:T(8,128)S(1)} fusion(bf16[1,3,128,1024]{3,0,2,1:T(2,128)(2,1)S(1)} %fusion.5), kind=kOutput, calls=%fused_computation.28 | convolution fusion | flops 821035008 | bytes 2359296 | tf_op jit(solution)/shard_map/dot_general | solution.py:61
  247.6 16.5 %fusion.42 = bf16[1,1,3,1,128,1024]{5,4,2,3,1,0:T(8,128)(2,1)S(1)} fusion(f32[3,128,1024]{2,1,0:T(8,128)S(1)} %fusion.21, bf16[1,3,128,1024]{3,0,2,1:T(2,128)(2,1)S(1)} %fusion.5), kind=kOutput, calls=%fused_computation.41 | convolution fusion | flops 821821440 | bytes 3145728 | tf_op jit(solution)/shard_map/dot_general | solution.py:64
  264.1 16.3 %fusion.39 = bf16[1,1,3,1,128,1024]{5,4,2,3,1,0:T(8,128)(2,1)S(1)} fusion(f32[3,128,1024]{2,1,0:T(8,128)S(1)} %fusion.23, bf16[1,3,128,1024]{3,0,2,1:T(2,128)(2,1)S(1)} %fusion.7), kind=kOutput, calls=%fused_computation.40 | convolution fusion | flops 821821440 | bytes 3145728 | tf_op jit(solution)/shard_map/dot_general | solution.py:61
  280.6 3.0 copy.44
  283.6 6.7 %all-to-all-start = ((bf16[2,1,3,1,128,1024]{4,0,3,2,1,5:T(2,128)(2,1)}), bf16[2,1,3,1,128,1024]{4,0,3,2,1,5:T(2,128)(2,1)S(1)}, u32[]{:S(2)}, u32[]{:S(2)}) async-start(bf16[2,1,3,1,128,1024]{4,0,3,2,1,5:T(2,128)(2,1)} %copy.44), calls=%async_computation | async-start | bytes 3145728 | tf_op jit(solution)/shard_map/all_to_all | solution.py:111
  290.4 22.9 %all-to-all-done = bf16[2,1,3,1,128,1024]{4,0,3,2,1,5:T(2,128)(2,1)S(1)} async-done(((bf16[2,1,3,1,128,1024]{4,0,3,2,1,5:T(2,128)(2,1)}), bf16[2,1,3,1,128,1024]{4,0,3,2,1,5:T(2,128)(2,1)S(1)}, u32[]{:S(2)}, u32[]{:S(2)}) %all-to-all-start) | async-done | bytes 1572896 | tf_op jit(solution)/shard_map/all_to_all | solution.py:111
  313.3 2.4 copy.45
  315.8 17.9 %fusion.29 = f32[1024,3,128]{2,0,1:T(8,128)S(1)} fusion(bf16[3,1024,128]{2,1,0:T(8,128)(2,1)S(1)} %bitcast.104), kind=kOutput, calls=%fused_computation.31 | convolution fusion | flops 821035008 | bytes 2359296 | tf_op jit(solution)/shard_map/wcxyk,yq->wcxqk/dot_general | solution.py:123
  333.7 18.0 %fusion.19 = f32[1024,3,128]{2,0,1:T(8,128)S(1)} fusion(bf16[3,1024,128]{2,1,0:T(8,128)(2,1)S(1)} %bitcast.105), kind=kOutput, calls=%fused_computation.26 | convolution fusion | flops 821035008 | bytes 2359296 | tf_op jit(solution)/shard_map/wcxyk,yq->wcxqk/dot_general | solution.py:122
  351.6 18.0 %fusion.17 = f32[1024,3,128]{2,0,1:T(8,128)S(1)} fusion(bf16[3,1024,128]{2,1,0:T(8,128)(2,1)S(1)} %bitcast.102), kind=kOutput, calls=%fused_computation.25 | convolution fusion | flops 821035008 | bytes 2359296 | tf_op jit(solution)/shard_map/wcxyk,yq->wcxqk/dot_general | solution.py:125
  369.6 18.0 %add_reduce_fusion = f32[1024,128]{1,0:T(8,128)S(1)} fusion(f32[1024,3,128]{2,0,1:T(8,128)S(1)} %fusion.29, f32[1024,3,128]{2,0,1:T(8,128)S(1)} %fusion.17, f32[1024,3,128]{2,0,1:T(8,128)S(1)} %fusion.19, bf16[3,1024,128]{2,1,0:T(8,128)(2,1)S(1)} %bitcast.103), kind=kOutput, calls=%fused_computation.36 | convolution fusion | flops 823263232 | bytes 6029312 | tf_op jit(solution)/shard_map/wcxyk,yq->wcxqk/dot_general | solution.py:120
  387.7 41.5 %while.14 = (s32[]{:T(128)}, f32[1,128]{1,0:T(1,128)S(1)}, f32[1,1024,128]{2,1,0:T(8,128)S(1)}, s32[1024,128]{1,0:T(8,128)}, s32[]{:T(128)}, /*index=5*/s32[]{:T(128)}, s32[]{:T(128)}, s32[]{:T(128)}) while((s32[]{:T(128)}, f32[1,128]{1,0:T(1,128)S(1)}, f32[1,1024,128]{2,1,0:T(8,128)S(1)}, s32[1024,128]{1,0:T(8,128)}, s32[]{:T(128)}, ...), condition=%wide.region_2.3_spmd.clone, body=%wide.region_1.2_spmd.clone.sunk | while | flops 13631751 | bytes 197789 | solution.py:144
  388.5 1.8 fusion.113
  393.7 1.8 fusion.113
  396.3 1.8 fusion.113
  398.9 1.8 fusion.113
  401.5 1.8 fusion.113
  429.3 75.6 %psum.7 = f32[8,128]{1,0:T(8,128)S(1)} all-reduce(f32[8,128]{1,0:T(8,128)S(1)} %broadcast_multiply_fusion), channel_id=1, replica_groups=mesh['tm'=32,'gy'=8] {'tm','gy'}, use_global_device_ids=true, to_apply=%region_3.4 | all-reduce | flops 1024 | bytes 8192 | tf_op jit(solution)/shard_map/psum | solution.py:152
  (77 shorter events, 39.6 us)
Async XLA Ops:
  7.2 8.7 %copy-start = (bf16[1,3,3,128,1024]{4,3,2,1,0:T(8,128)(2,1)S(1)}, bf16[1,3,3,128,1024]{4,3,2,1,0:T(8,128)(2,1)}, u32[]{:S(2)}) copy-start(bf16[1,3,3,128,1024]{4,3,2,1,0:T(8,128)(2,1)} %param.6) | copy-start | bytes 7077892
  7.2 158.9 %all-gather.2.cloned.1.call-start = ((), (), s32[]{:S(2)}) async-start(), calls=%async_computation.1 | async-start | bytes 25952256 | tf_op jit(solution)/shard_map/all_gather | solution.py:100
  8.5 8.2 %collective-permute-start = (bf16[1,2,1,1,1024]{4,3,2,1,0:T(2,128)(2,1)S(1)}, bf16[1,2,1,1,1024]{4,3,2,1,0:T(2,128)(2,1)S(1)}, u32[]{:S(2)}, u32[]{:S(2)}) collective-permute-start(bf16[1,2,1,1,1024]{4,3,2,1,0:T(2,128)(2,1)S(1)} %get-tuple-element.139), channel_id=1, source_target_pairs={{1,0},{2,1},{3,2},{4,3},{5,4},{6,5},{7,6},{0,7},{9,8},{10,9},{11,1... | collective-permute-start | bytes 12296 | tf_op jit(solution)/shard_map/ppermute | solution.py:23
  14.5 2.0 copy-start.2
  14.5 6.1 %collective-permute-start.1 = (bf16[1,2,1,1,1024]{4,3,2,1,0:T(2,128)(2,1)S(1)}, bf16[1,2,1,1,1024]{4,3,2,1,0:T(2,128)(2,1)S(1)}, u32[]{:S(2)}, u32[]{:S(2)}) collective-permute-start(bf16[1,2,1,1,1024]{4,3,2,1,0:T(2,128)(2,1)S(1)} %get-tuple-element.140), channel_id=1, source_target_pairs={{0,1},{1,2},{2,3},{3,4},{4,5},{5,6},{6,7},{7,0},{8,9},{9,10},{10,1... | collective-permute-start | bytes 12296 | tf_op jit(solution)/shard_map/ppermute | solution.py:21
  280.4 9.9 %copy-start.3 = (s32[9]{0:T(128)S(1)}, s32[9]{0:T(128)}, u32[]{:S(2)}) copy-start(s32[9]{0:T(128)} %param.9) | copy-start | bytes 112
  283.6 29.7 %all-to-all-start = ((bf16[2,1,3,1,128,1024]{4,0,3,2,1,5:T(2,128)(2,1)}), bf16[2,1,3,1,128,1024]{4,0,3,2,1,5:T(2,128)(2,1)S(1)}, u32[]{:S(2)}, u32[]{:S(2)}) async-start(bf16[2,1,3,1,128,1024]{4,0,3,2,1,5:T(2,128)(2,1)} %copy.44), calls=%async_computation | async-start | bytes 3145728 | tf_op jit(solution)/shard_map/all_to_all | solution.py:111
  429.2 76.3 %copy-start.1 = (f32[1,1024,128]{2,1,0:T(8,128)}, f32[1,1024,128]{2,1,0:T(8,128)S(1)}, u32[]{:S(2)}) copy-start(f32[1,1024,128]{2,1,0:T(8,128)S(1)} %get-tuple-element.195) | copy-start | bytes 1572868
Sparse Core Ops, SparseCore 0:
  23.8 142.1 all-gather.1
where the time goes:
time: 518 us; the launch traced here: 513 us
  matrix products  215 us (42%)
  waiting for transfers between devices  169 us (33%)
  blocking collectives  75.6 us (15%)
  local copies, waits for them, and re-layouts  19.7 us (4%)
  between operations  14.5 us (3%)
  starting transfers between devices  12.7 us (2%)
  other arithmetic  5.55 us (1%)
    all_gather x1, waiting for transfers between devices, body(): time_segment = lax.all_gather(electric, 'tm', axis=0, tiled=True)  142 us
    psum x1, blocking collectives, body(): binned = lax.psum(partial_value, ('tm', 'gy'))  75.6 us
    dot_general x16, matrix products, add_block(): return summed + jnp.dot(row_block, onehot, precision=highest)  28.7 us
    dot_general x1, matrix products, body(): jnp.einsum('wt,tcxyz->wcxyz', coefficient_real, time_segment, preferred_e...  24.9 us
    dot_general x1, matrix products, body(): jnp.einsum('wt,tcxyz->wcxyz', coefficient_imaginary, time_segment, prefer...  24.4 us
    all_to_all x1, waiting for transfers between devices, body(): lax.all_to_all(z_turn(re_part.astype(jnp.bfloat16), im_part.astype(jnp.bf...  22.9 us
    dot_general x1, matrix products, body(): jnp.einsum('wcxyk,yq->wcxqk', moved[0], ycos_tab, preferred_element_type=...  18 us
    dot_general x1, matrix products, body(): jnp.einsum('wcxyk,yq->wcxqk', moved[1], ysin_tab, preferred_element_type=...  18 us
  transfers between devices with their start and end apart: 4, of which 3 were waited for; matrix products, arithmetic and copies ran while one was open for 0% of the time, Pallas kernels for 0%

commit v1 on v0

--- a/solution.py
+++ b/solution.py
@@ -149,7 +149,8 @@
         (omega[None, :] >= omega_edges[:-1, None]) & (omega[None, :] < omega_edges[1:, None])
     ).astype(jnp.float32)
     partial_value = jnp.dot(member, by_mode, precision=highest)
-    binned = lax.psum(partial_value, ("tm", "gy"))
+    pieces = lax.all_gather(partial_value, ("tm", "gy"))
+    binned = jnp.sum(pieces, axis=0)
     spectrum = jnp.log(
         binned * (NB_W * bin_total) / (every_time_sample * y_count * z_count) + 1e-06
     )

time: 518 us -> 972 us (1.88)
  waiting for transfers between devices: 169 us -> 697 us
  blocking collectives: 75.6 us -> 0 us
    all_gather x0 -> x1, waiting for transfers between devices: none -> 528 us  [body(): pieces = lax.all_gather(partial_value, ('tm', 'gy'))]
    psum x1 -> x0, blocking collectives: 75.6 us -> none  [body(): binned = lax.psum(partial_value, ('tm', 'gy'))]
  transfers between devices with their start and end apart: 4 -> 5, of which waited for: 3 -> 4; matrix products, arithmetic and copies ran while one was open for 0% -> 0% of each run, Pallas kernels for 0% -> 0%
where the time goes in v1:
time: 972 us; the launch traced here: 967 us
  waiting for transfers between devices  697 us (72%)
  matrix products  215 us (22%)
  local copies, waits for them, and re-layouts  19.8 us (2%)
  between operations  14.5 us (1%)
  starting transfers between devices  12.5 us (1%)
    all_gather x1, waiting for transfers between devices, body(): pieces = lax.all_gather(partial_value, ('tm', 'gy'))  528 us
    all_gather x1, waiting for transfers between devices, body(): time_segment = lax.all_gather(electric, 'tm', axis=0, tiled=True)  142 us
    dot_general x16, matrix products, add_block(): return summed + jnp.dot(row_block, onehot, precision=highest)  28.7 us
    dot_general x1, matrix products, body(): jnp.einsum('wt,tcxyz->wcxyz', coefficient_real, time_segment, preferred_e...  24.9 us
    dot_general x1, matrix products, body(): jnp.einsum('wt,tcxyz->wcxyz', coefficient_imaginary, time_segment, prefer...  24.4 us
    all_to_all x1, waiting for transfers between devices, body(): lax.all_to_all(z_turn(re_part.astype(jnp.bfloat16), im_part.astype(jnp.bf...  22.9 us
  transfers between devices with their start and end apart: 5, of which 4 were waited for; matrix products, arithmetic and copies ran while one was open for 0% of the time, Pallas kernels for 0%

profile of v1, /device:TPU:1, one launch (start us, length us, event | category | flops | bytes accessed | tf_op | source)
XLA Modules:
  0.0 967.3 jit_solution(4561196361207591041)
XLA Ops:
  8.5 6.0 collective-permute-start
  16.7 3.9 collective-permute-done.1
  23.7 142.3 %all-gather.4.cloned.1.call-done = bf16[32,3,1,128,1024]{4,3,2,1,0:T(8,128)(2,1)} async-done(((bf16[1,3,1,128,1024]{4,3,2,1,0:T(8,128)(2,1)}), bf16[32,3,1,128,1024]{4,3,2,1,0:T(8,128)(2,1)}) %all-gather.4.cloned.1.call-update) | async-done | bytes 25165840 | tf_op jit(solution)/shard_map/all_gather | solution.py:100
  166.1 24.4 %fusion.5 = bf16[1,3,128,1024]{3,0,2,1:T(2,128)(2,1)S(1)} fusion(bf16[32,3,128,1024]{3,2,1,0:T(8,128)(2,1)} %bitcast.99, s32[]{:T(128)S(6)} %sub.139), kind=kOutput, calls=%fused_computation.8 | convolution fusion | flops 25166528 | bytes 25952260 | tf_op jit(solution)/shard_map/wt,tcxyz->wcxyz/dot_general | solution.py:108
  190.5 24.9 %fusion.7 = bf16[1,3,128,1024]{3,0,2,1:T(2,128)(2,1)S(1)} fusion(bf16[32,3,128,1024]{3,2,1,0:T(8,128)(2,1)} %bitcast.100, s32[]{:T(128)S(6)} %sub.139), kind=kOutput, calls=%fused_computation.10 | convolution fusion | flops 25166496 | bytes 25952260 | tf_op jit(solution)/shard_map/wt,tcxyz->wcxyz/dot_general | solution.py:105
  215.4 16.1 %fusion.21 = f32[3,128,1024]{2,1,0:T(8,128)S(1)} fusion(bf16[1,3,128,1024]{3,0,2,1:T(2,128)(2,1)S(1)} %fusion.7), kind=kOutput, calls=%fused_computation.27 | convolution fusion | flops 821035008 | bytes 2359296 | tf_op jit(solution)/shard_map/dot_general | solution.py:64
  231.5 16.1 %fusion.23 = f32[3,128,1024]{2,1,0:T(8,128)S(1)} fusion(bf16[1,3,128,1024]{3,0,2,1:T(2,128)(2,1)S(1)} %fusion.5), kind=kOutput, calls=%fused_computation.28 | convolution fusion | flops 821035008 | bytes 2359296 | tf_op jit(solution)/shard_map/dot_general | solution.py:61
  247.6 16.5 %fusion.42 = bf16[1,1,3,1,128,1024]{5,4,2,3,1,0:T(8,128)(2,1)S(1)} fusion(f32[3,128,1024]{2,1,0:T(8,128)S(1)} %fusion.21, bf16[1,3,128,1024]{3,0,2,1:T(2,128)(2,1)S(1)} %fusion.5), kind=kOutput, calls=%fused_computation.41 | convolution fusion | flops 821821440 | bytes 3145728 | tf_op jit(solution)/shard_map/dot_general | solution.py:64
  264.1 16.3 %fusion.39 = bf16[1,1,3,1,128,1024]{5,4,2,3,1,0:T(8,128)(2,1)S(1)} fusion(f32[3,128,1024]{2,1,0:T(8,128)S(1)} %fusion.23, bf16[1,3,128,1024]{3,0,2,1:T(2,128)(2,1)S(1)} %fusion.7), kind=kOutput, calls=%fused_computation.40 | convolution fusion | flops 821821440 | bytes 3145728 | tf_op jit(solution)/shard_map/dot_general | solution.py:61
  280.6 3.0 copy.54
  283.6 6.4 all-to-all-start
  290.2 22.9 %all-to-all-done = bf16[2,1,3,1,128,1024]{4,0,3,2,1,5:T(2,128)(2,1)S(1)} async-done(((bf16[2,1,3,1,128,1024]{4,0,3,2,1,5:T(2,128)(2,1)}), bf16[2,1,3,1,128,1024]{4,0,3,2,1,5:T(2,128)(2,1)S(1)}, u32[]{:S(2)}, u32[]{:S(2)}) %all-to-all-start) | async-done | bytes 1572896 | tf_op jit(solution)/shard_map/all_to_all | solution.py:111
  313.1 2.6 copy.55
  315.7 17.9 %fusion.29 = f32[1024,3,128]{2,0,1:T(8,128)S(1)} fusion(bf16[3,1024,128]{2,1,0:T(8,128)(2,1)S(1)} %bitcast.106), kind=kOutput, calls=%fused_computation.31 | convolution fusion | flops 821035008 | bytes 2359296 | tf_op jit(solution)/shard_map/wcxyk,yq->wcxqk/dot_general | solution.py:123
  333.6 18.0 %fusion.19 = f32[1024,3,128]{2,0,1:T(8,128)S(1)} fusion(bf16[3,1024,128]{2,1,0:T(8,128)(2,1)S(1)} %bitcast.107), kind=kOutput, calls=%fused_computation.26 | convolution fusion | flops 821035008 | bytes 2359296 | tf_op jit(solution)/shard_map/wcxyk,yq->wcxqk/dot_general | solution.py:122
  351.6 18.0 %fusion.17 = f32[1024,3,128]{2,0,1:T(8,128)S(1)} fusion(bf16[3,1024,128]{2,1,0:T(8,128)(2,1)S(1)} %bitcast.104), kind=kOutput, calls=%fused_computation.25 | convolution fusion | flops 821035008 | bytes 2359296 | tf_op jit(solution)/shard_map/wcxyk,yq->wcxqk/dot_general | solution.py:125
  369.6 18.0 %add_reduce_fusion = f32[1024,128]{1,0:T(8,128)S(1)} fusion(f32[1024,3,128]{2,0,1:T(8,128)S(1)} %fusion.29, f32[1024,3,128]{2,0,1:T(8,128)S(1)} %fusion.17, f32[1024,3,128]{2,0,1:T(8,128)S(1)} %fusion.19, bf16[3,1024,128]{2,1,0:T(8,128)(2,1)S(1)} %bitcast.105), kind=kOutput, calls=%fused_computation.36 | convolution fusion | flops 823263232 | bytes 6029312 | tf_op jit(solution)/shard_map/wcxyk,yq->wcxqk/dot_general | solution.py:120
  387.7 41.5 %while.14 = (s32[]{:T(128)}, f32[1,128]{1,0:T(1,128)S(1)}, f32[1,1024,128]{2,1,0:T(8,128)S(1)}, s32[1024,128]{1,0:T(8,128)}, s32[]{:T(128)}, /*index=5*/s32[]{:T(128)}, s32[]{:T(128)}, s32[]{:T(128)}) while((s32[]{:T(128)}, f32[1,128]{1,0:T(1,128)S(1)}, f32[1,1024,128]{2,1,0:T(8,128)S(1)}, s32[1024,128]{1,0:T(8,128)}, s32[]{:T(128)}, ...), condition=%wide.region_2.3_spmd.clone, body=%wide.region_1.2_spmd.clone.sunk | while | flops 13631751 | bytes 197789 | solution.py:144
  391.1 1.8 fusion.113
  393.7 1.8 fusion.113
  396.2 1.8 fusion.113
  398.8 1.8 fusion.113
  401.4 1.8 fusion.113
  429.9 528.2 %all-gather.6.cloned.1.call-done = f32[2048,128]{1,0:T(8,128)} async-done(((f32[8,128]{1,0:T(8,128)}), f32[2048,128]{1,0:T(8,128)}) %all-gather.6.cloned.1.call-update) | async-done | bytes 1048592 | tf_op jit(solution)/shard_map/all_gather | solution.py:152
  (80 shorter events, 41.8 us)
Async XLA Ops:
  7.2 8.7 copy-start
  7.2 158.9 %all-gather.4.cloned.1.call-start = ((), (), s32[]{:S(2)}) async-start(), calls=%async_computation.1 | async-start | bytes 25952256 | tf_op jit(solution)/shard_map/all_gather | solution.py:100
  8.5 8.2 collective-permute-start
  14.5 2.0 copy-start.2
  14.5 6.1 collective-permute-start.1
  280.4 9.7 %copy-start.3 = (s32[9]{0:T(128)S(1)}, s32[9]{0:T(128)}, u32[]{:S(2)}) copy-start(s32[9]{0:T(128)} %param.9) | copy-start | bytes 112
  283.6 29.4 %all-to-all-start = ((bf16[2,1,3,1,128,1024]{4,0,3,2,1,5:T(2,128)(2,1)}), bf16[2,1,3,1,128,1024]{4,0,3,2,1,5:T(2,128)(2,1)S(1)}, u32[]{:S(2)}, u32[]{:S(2)}) async-start(bf16[2,1,3,1,128,1024]{4,0,3,2,1,5:T(2,128)(2,1)} %copy.54), calls=%async_computation | async-start | bytes 3145728 | tf_op jit(solution)/shard_map/all_to_all | solution.py:111
  290.1 668.0 %all-gather.6.cloned.1.call-start = ((), (), s32[]{:S(2)}) async-start(), calls=%async_computation.2 | async-start | bytes 1052672 | tf_op jit(solution)/shard_map/all_gather | solution.py:152
  429.1 531.1 %copy-start.1 = (f32[1,1024,128]{2,1,0:T(8,128)}, f32[1,1024,128]{2,1,0:T(8,128)S(1)}, u32[]{:S(2)}) copy-start(f32[1,1024,128]{2,1,0:T(8,128)S(1)} %get-tuple-element.197) | copy-start | bytes 1572868
Sparse Core Ops, SparseCore 0:
  23.8 142.1 all-gather.3
  430.1 527.9 all-gather.5
